TPU v7x, 32 devices: a whole 2x2x4 slice. The times are simulated.
32 devices in a mesh: dom: 8 (over y, x, core), head: 4 (over z).
Axes of the slice: x: 2, y: 2, z: 4, core: 2. Of those that a mesh axis runs over, the one named last changes fastest.
Arguments:
- features: bfloat16 [25, 128, 4096], P(None, None, ('dom', 'head')), may hold values from -14 to 14
- positions: float32 [3, 4096], P(None, 'dom'), may hold values from 0 to 3
- penalty: float32 [16], replicated, may hold values from 0.01 to 0.5
- qk_weight: bfloat16 [128, 2048], replicated, may hold values from -0.5 to 0.5
- value_weight: bfloat16 [5, 128, 128], replicated, may hold values from -0.5 to 0.5
- output_weight: bfloat16 [5, 128, 128], replicated, may hold values from -0.5 to 0.5
- frames: float32 [64, 25, 25], replicated, may hold values from -3 to 3, as said below
- frame_index: int32 [64], P('dom'), may hold values from 0 to 63
- neighbours: int32 [64, 8], P('dom'), may hold values from 0 to 63, as said below
- counts: int32 [64], P('dom'), may hold values from 1 to 8
- cotangent: bfloat16 [25, 128, 4096], P(None, None, ('dom', 'head')), may hold values from -6 to 6
Outputs:
- updated: bfloat16 [25, 128, 4096], P(None, None, ('dom', 'head'))
- forces: float32 [3, 4096], P(None, ('dom', 'head'))
Inputs may be any that keep to these rules, and one draw needn't show every extreme that they name: `frames`: entries outside the diagonal blocks of components of one degree are zero. `neighbours`: row b holds 8 distinct blocks (b + o) mod 64 with |o| <= 4; the slots at and beyond counts[b] are padding.
All inputs are finite; a program needn't handle non-finite values.
Results may differ from a plain program's by a relative error of at most 0.0037.
The roundings to bfloat16 on the way count: a program that leaves them out, or rounds other values in their place, can miss the bound.
Values may be sent and summed in bfloat16 or wider, within the bound.
A program may use at most 64 MiB of HBM per device.

v0:
```python
import math
import jax
import jax.numpy as jnp
from jax import lax
from jax.sharding import PartitionSpec as P

COMP = 25
LDEG = 5
HEADS = 16
ALPHA = 64
BLOCK = 64
NBR = 8
REACH = 4
NFRAME = 64
NEG_FILL = -1e30


def extended(shard, sides, width):
    for axis, dim in sides:
        peers, length = (lax.axis_size(axis), shard.shape[dim])
        up = [(i, (i + 1) % peers) for i in range(peers)]
        down = [(j, i) for i, j in up]
        last = lax.slice_in_dim(shard, length - width, length, axis=dim)
        initial = lax.slice_in_dim(shard, 0, width, axis=dim)
        before = lax.ppermute(last, axis, up)
        after = lax.ppermute(initial, axis, down)
        shard = jnp.concatenate([before, shard, after], axis=dim)
    return shard


def from_behind(shard, axis, by):
    peers = lax.axis_size(axis)
    return lax.ppermute(shard, axis, [(i, (i + by) % peers) for i in range(peers)])


def degree_table():
    components = jnp.arange(COMP)
    degrees = jnp.sum(
        (components[:, None] >= (jnp.arange(1, LDEG) ** 2)[None, :]).astype(jnp.int32), axis=1
    )
    orders = components - degrees * degrees - degrees
    return (jnp.abs(orders) <= 2).astype(jnp.float32)


def projectors(frames):
    kept_mask = degree_table()
    return jnp.einsum("fji,j,fjk->fik", frames, kept_mask, frames, precision=lax.Precision.HIGHEST)


def mix_degrees(operand, weights, reverse):
    pieces = []
    for degree in range(weights.shape[0]):
        sliced = operand[degree * degree : (degree + 1) * (degree + 1)]
        if reverse:
            pieces.append(
                jnp.einsum(
                    "koa,co->kca", sliced, weights[degree], preferred_element_type=jnp.float32
                )
            )
        else:
            pieces.append(
                jnp.einsum(
                    "kca,co->koa", sliced, weights[degree], preferred_element_type=jnp.float32
                )
            )
    return jnp.concatenate(pieces, 0)


def pick_group(nblocks, heads_here):
    chosen = 1
    for candidate in range(1, nblocks + 1):
        if nblocks % candidate == 0 and candidate * BLOCK * heads_here <= 512:
            chosen = candidate
    return chosen


def block_meta(neighbours, counts, frame_index, projections, first_block, total_blocks):
    local_index = jnp.mod(neighbours - first_block + REACH, total_blocks)
    usable = jnp.arange(NBR)[None, :] < counts[:, None]
    onehot = (frame_index[:, None] == jnp.arange(NFRAME)[None, :]).astype(jnp.float32)
    matrices = jnp.dot(
        onehot, projections.reshape(NFRAME, COMP * COMP), precision=lax.Precision.HIGHEST
    )
    return (local_index, usable, matrices.reshape(-1, COMP, COMP))


def attend(
    queries,
    keys_ext,
    values_ext,
    grads,
    own_points,
    ext_points,
    penalty_here,
    local_index,
    usable,
    matrices,
):
    heads_here = penalty_here.shape[0]
    head_width = values_ext.shape[1] // heads_here
    query_blocks_count = queries.shape[1] // BLOCK
    ext_blocks = keys_ext.shape[1] // BLOCK
    query_blocks = queries.reshape(heads_here, ALPHA, query_blocks_count, BLOCK)
    key_blocks = keys_ext.reshape(heads_here, ALPHA, ext_blocks, BLOCK)
    value_blocks = values_ext.reshape(COMP, heads_here, head_width, ext_blocks, BLOCK)
    grad_blocks = grads.reshape(COMP, heads_here, head_width, query_blocks_count, BLOCK)
    own_blocks = own_points.reshape(3, query_blocks_count, BLOCK)
    ext_point_blocks = ext_points.reshape(3, ext_blocks, BLOCK)
    group_size = pick_group(query_blocks_count, heads_here)
    inverse_root = 1.0 / math.sqrt(ALPHA)
    block_range = jnp.arange(ext_blocks)

    def group_step(state_now, begin_at):
        attended_all, query_forces, ghost_forces = state_now
        slot_blocks = lax.dynamic_slice_in_dim(local_index, begin_at, group_size, 0)
        query_group = lax.dynamic_slice_in_dim(query_blocks, begin_at, group_size, 2)
        key_group = jnp.take(key_blocks, slot_blocks, axis=2)
        value_group = jnp.take(value_blocks, slot_blocks, axis=3)
        grad_group = lax.dynamic_slice_in_dim(grad_blocks, begin_at, group_size, 3)
        query_points = lax.dynamic_slice_in_dim(own_blocks, begin_at, group_size, 1)
        key_points = jnp.take(ext_point_blocks, slot_blocks, axis=1)
        live_slots = lax.dynamic_slice_in_dim(usable, begin_at, group_size, 0)
        group_mats = lax.dynamic_slice_in_dim(matrices, begin_at, group_size, 0)
        scores = (
            jnp.einsum(
                "hagi,hagsj->hgisj", query_group, key_group, preferred_element_type=jnp.float32
            )
            * inverse_root
        )
        separation = query_points[:, :, :, None, None] - key_points[:, :, None, :, :]
        distance = jnp.sum(separation * separation, axis=0)
        logits = scores - penalty_here[:, None, None, None, None] * distance[None]
        slot_mask = live_slots[None, :, None, :, None]
        logits = jnp.where(slot_mask, logits, NEG_FILL)
        peaks = jnp.max(logits, axis=(3, 4), keepdims=True)
        exponent = jnp.where(slot_mask, jnp.exp(logits - peaks), 0.0)
        attention = exponent / jnp.sum(exponent, axis=(3, 4), keepdims=True)
        rounded = attention.astype(jnp.bfloat16)
        aggregate = jnp.einsum(
            "hgisj,khdgsj->khdgi", rounded, value_group, preferred_element_type=jnp.float32
        )
        attended = jnp.einsum(
            "gkl,lhdgi->khdgi", group_mats, aggregate, precision=lax.Precision.HIGHEST
        ).astype(jnp.bfloat16)
        rotated = jnp.einsum(
            "glk,lhdgi->khdgi",
            group_mats,
            grad_group.astype(jnp.float32),
            precision=lax.Precision.HIGHEST,
        ).astype(jnp.bfloat16)
        weight_grads = jnp.einsum(
            "khdgi,khdgsj->hgisj", rotated, value_group, preferred_element_type=jnp.float32
        )
        logit_grads = attention * (
            weight_grads - jnp.sum(attention * weight_grads, axis=(3, 4), keepdims=True)
        )
        total = jnp.sum(2.0 * penalty_here[:, None, None, None, None] * logit_grads, axis=0)
        force_query = jnp.sum(total[None] * separation, axis=(3, 4))
        force_key = -jnp.sum(total[None] * separation, axis=2)
        onehot = (slot_blocks[:, :, None] == block_range[None, None, :]).astype(jnp.float32)
        ghost_forces = ghost_forces + jnp.einsum(
            "gse,cgsj->cej", onehot, force_key, precision=lax.Precision.HIGHEST
        )
        attended_all = lax.dynamic_update_slice_in_dim(attended_all, attended, begin_at, 3)
        query_forces = lax.dynamic_update_slice_in_dim(query_forces, force_query, begin_at, 1)
        return ((attended_all, query_forces, ghost_forces), None)

    initial = (
        jnp.zeros((COMP, heads_here, head_width, query_blocks_count, BLOCK), jnp.bfloat16),
        jnp.zeros((3, query_blocks_count, BLOCK), jnp.float32),
        jnp.zeros((3, ext_blocks, BLOCK), jnp.float32),
    )
    begins = jnp.arange(0, query_blocks_count, group_size)
    final_state, unused_out = lax.scan(group_step, initial, begins)
    attended_all, query_forces, ghost_forces = final_state
    return (
        attended_all.reshape(COMP, heads_here * head_width, query_blocks_count * BLOCK),
        query_forces.reshape(3, query_blocks_count * BLOCK),
        ghost_forces.reshape(3, ext_blocks * BLOCK),
    )


def on_device(
    features,
    positions,
    penalty,
    qk_weight,
    value_weight,
    output_weight,
    frames,
    frame_index,
    neighbours,
    counts,
    cotangent,
):
    atoms_here = features.shape[2]
    halo_width = REACH * BLOCK
    query_rows = HEADS * ALPHA
    projections = projectors(frames)
    grads = mix_degrees(cotangent, output_weight, True).astype(jnp.bfloat16)
    pos_ext = extended(positions, (("dom", 1),), halo_width)
    dom_atoms = positions.shape[1]
    dom_blocks = dom_atoms // BLOCK
    dom_count = lax.axis_size("dom")
    head_count = lax.axis_size("head")
    queries_keys = lax.dot_general(
        qk_weight, features[0], (((0,), (0,)), ((), ())), preferred_element_type=jnp.float32
    ).astype(jnp.bfloat16)
    values = mix_degrees(features, value_weight, False).astype(jnp.bfloat16)
    heads_here = HEADS // head_count
    paired = queries_keys.reshape(2, query_rows, atoms_here)
    paired_heads, values_heads, grads_heads = (
        lax.all_to_all(paired, "head", split_axis=1, concat_axis=2, tiled=True),
        lax.all_to_all(values, "head", split_axis=1, concat_axis=2, tiled=True),
        lax.all_to_all(grads, "head", split_axis=1, concat_axis=2, tiled=True),
    )
    packed = jnp.concatenate([paired_heads[1], values_heads.reshape(-1, dom_atoms)], 0)
    packed_ext = extended(packed, (("dom", 1),), halo_width)
    key_rows = heads_here * ALPHA
    penalty_here = lax.dynamic_slice_in_dim(
        penalty, lax.axis_index("head") * heads_here, heads_here
    )
    local_index, usable, matrices = block_meta(
        neighbours,
        counts,
        frame_index,
        projections,
        lax.axis_index("dom") * dom_blocks,
        dom_count * dom_blocks,
    )
    attended_all, force_query, force_ext = attend(
        paired_heads[0],
        packed_ext[:key_rows],
        packed_ext[key_rows:].reshape(COMP, -1, dom_atoms + 2 * halo_width),
        grads_heads,
        pos_ext[:, halo_width : halo_width + dom_atoms],
        pos_ext,
        penalty_here,
        local_index,
        usable,
        matrices,
    )
    attended_atoms = lax.all_to_all(attended_all, "head", split_axis=2, concat_axis=1, tiled=True)
    force_dom = force_query + force_ext[:, halo_width : halo_width + dom_atoms]
    for offset in (-1, 1):
        if offset < 0:
            rim_part = force_ext[:, :halo_width]
        else:
            rim_part = force_ext[:, halo_width + dom_atoms :]
        arrived = from_behind(rim_part, "dom", offset)
        if offset < 0:
            force_dom = force_dom.at[:, dom_atoms - halo_width :].add(arrived)
        else:
            force_dom = force_dom.at[:, :halo_width].add(arrived)
    forces = lax.psum_scatter(force_dom, "head", scatter_dimension=1, tiled=True)
    updated = (
        features.astype(jnp.float32) + mix_degrees(attended_atoms, output_weight, False)
    ).astype(jnp.bfloat16)
    return (updated, forces)


def solution(mesh):
    in_specs = (
        P(None, None, ("dom", "head")),
        P(None, "dom"),
        P(),
        P(),
        P(),
        P(),
        P(),
        P("dom"),
        P("dom", None),
        P("dom"),
        P(None, None, ("dom", "head")),
    )
    out_specs = (P(None, None, ("dom", "head")), P(None, ("dom", "head")))
    return jax.shard_map(
        on_device, mesh=mesh, in_specs=in_specs, out_specs=out_specs, check_vma=False
    )
```

profile of v0, /device:TPU:0, one launch (start us, length us, event | category | flops | bytes accessed | tf_op | source)
XLA Modules:
  0.0 372.3 jit_solution(10311147214418356075)
XLA Ops:
  10.7 6.3 %all-to-all-start = ((bf16[2,1024,128]{2,0,1:T(2,128)(2,1)}), bf16[2,1024,128]{2,0,1:T(2,128)(2,1)S(1)}, u32[]{:S(2)}, u32[]{:S(2)}) async-start(bf16[2,1024,128]{2,0,1:T(2,128)(2,1)} %copy.174), calls=%async_computation | async-start | bytes 1048576 | tf_op jit(solution)/shard_map/all_to_all | solution.py:213
  17.1 2.6 collective-permute-start.3
  21.1 1.5 copy.181
  23.3 8.2 %all-to-all-done = bf16[2,1024,128]{2,0,1:T(2,128)(2,1)S(1)} async-done(((bf16[2,1024,128]{2,0,1:T(2,128)(2,1)}), bf16[2,1024,128]{2,0,1:T(2,128)(2,1)S(1)}, u32[]{:S(2)}, u32[]{:S(2)}) %all-to-all-start) | async-done | bytes 524320 | tf_op jit(solution)/shard_map/all_to_all | solution.py:213
  31.5 4.3 %all-to-all-start.1 = ((bf16[25,128,128]{2,0,1:T(8,128)(2,1)}), bf16[25,128,128]{2,0,1:T(8,128)(2,1)}, u32[]{:S(2)}, u32[]{:S(2)}) async-start(bf16[25,128,128]{2,0,1:T(8,128)(2,1)} %copy.181), calls=%async_computation.1 | async-start | bytes 2097152 | tf_op jit(solution)/shard_map/all_to_all | solution.py:214
  36.1 1.5 copy.188
  38.8 1.8 copy.185
  40.6 2.4 convolution_bitcast_fusion.1
  43.0 18.1 %all-to-all-done.1 = bf16[25,128,128]{2,0,1:T(8,128)(2,1)} async-done(((bf16[25,128,128]{2,0,1:T(8,128)(2,1)}), bf16[25,128,128]{2,0,1:T(8,128)(2,1)}, u32[]{:S(2)}, u32[]{:S(2)}) %all-to-all-start.1) | async-done | bytes 819232 | tf_op jit(solution)/shard_map/all_to_all | solution.py:214
  61.1 3.5 all-to-all-start.2
  65.8 1.9 copy.182
  68.9 2.6 collective-permute-start.1
  71.7 1.5 copy.187
  74.3 1.6 fusion.105
  78.3 11.6 %all-to-all-done.2 = bf16[25,128,128]{2,0,1:T(8,128)(2,1)S(1)} async-done(((bf16[25,128,128]{2,0,1:T(8,128)(2,1)}), bf16[25,128,128]{2,0,1:T(8,128)(2,1)S(1)}, u32[]{:S(2)}, u32[]{:S(2)}) %all-to-all-start.2) | async-done | bytes 819232 | tf_op jit(solution)/shard_map/all_to_all | solution.py:215
  90.6 1.6 reshape.146
  95.8 3.4 reshape_reshape.3
  99.2 5.2 %copy.190 = bf16[25,4,8,16,64]{4,2,3,1,0:T(8,128)(2,1)} copy(bf16[25,4,8,16,64]{4,3,2,1,0:T(8,128)(2,1)} %reshape_reshape.3) | data formatting | bytes 3276800
  104.3 1.6 broadcast_in_dim.78.clone
  106.0 200.0 %while.17 = (s32[]{:T(128)}, bf16[25,4,8,8,64]{4,3,2,1,0:T(8,128)(2,1)}, f32[3,8,64]{2,1,0:T(8,128)S(1)}, f32[3,16,64]{2,1,0:T(8,128)S(1)}, s32[4]{0:T(128)S(1)}...) while((s32[]{:T(128)}, ...), condition=%wide.region_9.10_spmd.clone, body=%wide.region_1.9_spmd.clone.sunk | while | flops 315474432 | bytes 35243308 | solution.py:174
  115.2 1.9 constant_dynamic-slice_fusion.13
  118.1 5.3 %gather_fusion.2 = bf16[16,25,4,8,64]{4,3,2,1,0:T(8,128)(2,1)} fusion(bf16[25,4,8,16,64]{4,2,3,1,0:T(8,128)(2,1)} %get-tuple-element.472, s32[1024]{0:T(1024)S(1)} %pad_clamp_fusion.2), kind=kCustom, calls=%fused_computation.clone.clone.1 | custom fusion | bytes 3276864 | tf_op jit(solution)/shard_map/while/body/eval_jaxpr/jit(_take)/gather | solution.py:118
  123.4 4.2 %fusion.158 = (f32[4,2,64]{2,1,0:T(2,128)S(1)}, f32[4,2,64,8,64]{2,4,3,1,0:T(8,128)S(1)}, f32[4,2,64,8,64,1]{2,4,5,3,1,0:T(8,128)S(1)}) fusion(f32[4,2,64]{2,1,0:T(2,128)S(1)} %fusion.156, f32[4,2,64]{2,1,0:T(2,128)S(1)} %get-tuple-element.422, f32[2,64,8,64]{1,3,2,0:T(8,128)S(1)} %copy.287, f32[4]{0:T(128)S(1)} %get-tuple-element.476, ...), kind=kOutput, calls=%fused_computation.14.clone.1 | convolution fusion | flops 108035584 | bytes 5257264 | tf_op jit(solution)/shard_map/while/body/eval_jaxpr/khdgi,khdgsj->hgisj/dot_general | solution.py:151
  129.5 2.2 fusion.160
  133.2 21.0 %dynamic_update_slice.10 = bf16[25,4,8,8,64]{4,3,2,1,0:T(8,128)(2,1)} dynamic-update-slice(bf16[25,4,8,8,64]{4,3,2,1,0:T(8,128)(2,1)} %get-tuple-element.449, bf16[25,4,8,2,64]{4,3,2,1,0:T(2,128)(2,1)S(1)} %copy.289, s32[]{:T(128)} %constant.140.clone.1..sunk, s32[]{:T(128)} %constant.140.clone.1..sunk, s32[]{:T(128)} %constant.140.clone.1..sunk, s32[]{:T(128)S(6)} %select_n.111, ...) | dynamic-update-slice | bytes 409604 | tf_op jit(solution)/shard_map/while/body/eval_jaxpr/dynamic_update_slice | solution.py:164
  165.2 1.9 constant_dynamic-slice_fusion.13
  168.1 5.3 %gather_fusion.2 = bf16[16,25,4,8,64]{4,3,2,1,0:T(8,128)(2,1)} fusion(bf16[25,4,8,16,64]{4,2,3,1,0:T(8,128)(2,1)} %get-tuple-element.472, s32[1024]{0:T(1024)S(1)} %pad_clamp_fusion.2), kind=kCustom, calls=%fused_computation.clone.clone.1 | custom fusion | bytes 3276864 | tf_op jit(solution)/shard_map/while/body/eval_jaxpr/jit(_take)/gather | solution.py:118
  173.4 4.2 %fusion.158 = (f32[4,2,64]{2,1,0:T(2,128)S(1)}, f32[4,2,64,8,64]{2,4,3,1,0:T(8,128)S(1)}, f32[4,2,64,8,64,1]{2,4,5,3,1,0:T(8,128)S(1)}) fusion(f32[4,2,64]{2,1,0:T(2,128)S(1)} %fusion.156, f32[4,2,64]{2,1,0:T(2,128)S(1)} %get-tuple-element.422, f32[2,64,8,64]{1,3,2,0:T(8,128)S(1)} %copy.287, f32[4]{0:T(128)S(1)} %get-tuple-element.476, ...), kind=kOutput, calls=%fused_computation.14.clone.1 | convolution fusion | flops 108035584 | bytes 5257264 | tf_op jit(solution)/shard_map/while/body/eval_jaxpr/khdgi,khdgsj->hgisj/dot_general | solution.py:151
  179.5 2.2 fusion.160
  183.2 21.0 %dynamic_update_slice.10 = bf16[25,4,8,8,64]{4,3,2,1,0:T(8,128)(2,1)} dynamic-update-slice(bf16[25,4,8,8,64]{4,3,2,1,0:T(8,128)(2,1)} %get-tuple-element.449, bf16[25,4,8,2,64]{4,3,2,1,0:T(2,128)(2,1)S(1)} %copy.289, s32[]{:T(128)} %constant.140.clone.1..sunk, s32[]{:T(128)} %constant.140.clone.1..sunk, s32[]{:T(128)} %constant.140.clone.1..sunk, s32[]{:T(128)S(6)} %select_n.111, ...) | dynamic-update-slice | bytes 409604 | tf_op jit(solution)/shard_map/while/body/eval_jaxpr/dynamic_update_slice | solution.py:164
  215.2 1.9 constant_dynamic-slice_fusion.13
  218.1 5.3 %gather_fusion.2 = bf16[16,25,4,8,64]{4,3,2,1,0:T(8,128)(2,1)} fusion(bf16[25,4,8,16,64]{4,2,3,1,0:T(8,128)(2,1)} %get-tuple-element.472, s32[1024]{0:T(1024)S(1)} %pad_clamp_fusion.2), kind=kCustom, calls=%fused_computation.clone.clone.1 | custom fusion | bytes 3276864 | tf_op jit(solution)/shard_map/while/body/eval_jaxpr/jit(_take)/gather | solution.py:118
  223.4 4.2 %fusion.158 = (f32[4,2,64]{2,1,0:T(2,128)S(1)}, f32[4,2,64,8,64]{2,4,3,1,0:T(8,128)S(1)}, f32[4,2,64,8,64,1]{2,4,5,3,1,0:T(8,128)S(1)}) fusion(f32[4,2,64]{2,1,0:T(2,128)S(1)} %fusion.156, f32[4,2,64]{2,1,0:T(2,128)S(1)} %get-tuple-element.422, f32[2,64,8,64]{1,3,2,0:T(8,128)S(1)} %copy.287, f32[4]{0:T(128)S(1)} %get-tuple-element.476, ...), kind=kOutput, calls=%fused_computation.14.clone.1 | convolution fusion | flops 108035584 | bytes 5257264 | tf_op jit(solution)/shard_map/while/body/eval_jaxpr/khdgi,khdgsj->hgisj/dot_general | solution.py:151
  229.5 2.2 fusion.160
  233.2 21.0 %dynamic_update_slice.10 = bf16[25,4,8,8,64]{4,3,2,1,0:T(8,128)(2,1)} dynamic-update-slice(bf16[25,4,8,8,64]{4,3,2,1,0:T(8,128)(2,1)} %get-tuple-element.449, bf16[25,4,8,2,64]{4,3,2,1,0:T(2,128)(2,1)S(1)} %copy.289, s32[]{:T(128)} %constant.140.clone.1..sunk, s32[]{:T(128)} %constant.140.clone.1..sunk, s32[]{:T(128)} %constant.140.clone.1..sunk, s32[]{:T(128)S(6)} %select_n.111, ...) | dynamic-update-slice | bytes 409604 | tf_op jit(solution)/shard_map/while/body/eval_jaxpr/dynamic_update_slice | solution.py:164
  265.2 1.9 constant_dynamic-slice_fusion.13
  268.1 5.3 %gather_fusion.2 = bf16[16,25,4,8,64]{4,3,2,1,0:T(8,128)(2,1)} fusion(bf16[25,4,8,16,64]{4,2,3,1,0:T(8,128)(2,1)} %get-tuple-element.472, s32[1024]{0:T(1024)S(1)} %pad_clamp_fusion.2), kind=kCustom, calls=%fused_computation.clone.clone.1 | custom fusion | bytes 3276864 | tf_op jit(solution)/shard_map/while/body/eval_jaxpr/jit(_take)/gather | solution.py:118
  273.4 4.2 %fusion.158 = (f32[4,2,64]{2,1,0:T(2,128)S(1)}, f32[4,2,64,8,64]{2,4,3,1,0:T(8,128)S(1)}, f32[4,2,64,8,64,1]{2,4,5,3,1,0:T(8,128)S(1)}) fusion(f32[4,2,64]{2,1,0:T(2,128)S(1)} %fusion.156, f32[4,2,64]{2,1,0:T(2,128)S(1)} %get-tuple-element.422, f32[2,64,8,64]{1,3,2,0:T(8,128)S(1)} %copy.287, f32[4]{0:T(128)S(1)} %get-tuple-element.476, ...), kind=kOutput, calls=%fused_computation.14.clone.1 | convolution fusion | flops 108035584 | bytes 5257264 | tf_op jit(solution)/shard_map/while/body/eval_jaxpr/khdgi,khdgsj->hgisj/dot_general | solution.py:151
  279.5 2.2 fusion.160
  283.2 21.0 %dynamic_update_slice.10 = bf16[25,4,8,8,64]{4,3,2,1,0:T(8,128)(2,1)} dynamic-update-slice(bf16[25,4,8,8,64]{4,3,2,1,0:T(8,128)(2,1)} %get-tuple-element.449, bf16[25,4,8,2,64]{4,3,2,1,0:T(2,128)(2,1)S(1)} %copy.289, s32[]{:T(128)} %constant.140.clone.1..sunk, s32[]{:T(128)} %constant.140.clone.1..sunk, s32[]{:T(128)} %constant.140.clone.1..sunk, s32[]{:T(128)S(6)} %select_n.111, ...) | dynamic-update-slice | bytes 409604 | tf_op jit(solution)/shard_map/while/body/eval_jaxpr/dynamic_update_slice | solution.py:164
  306.0 3.0 reshape.147
  309.0 6.5 %copy.197 = bf16[25,32,512]{1,0,2:T(8,128)(2,1)} copy(bf16[25,32,512]{2,1,0:T(8,128)(2,1)S(1)} %reshape.147) | data formatting | bytes 1638400 | tf_op jit(solution)/shard_map/reshape | solution.py:177
  315.5 5.3 %reshape.212 = bf16[4,2,51200]{2,1,0:T(2,128)(2,1)} reshape(bf16[512,25,32]{2,1,0:T(8,128)(2,1)} %bitcast.289) | data formatting | bytes 1638400
  320.8 3.6 all-to-all-start.3
  327.8 2.6 collective-permute-done.5
  332.9 18.3 %reduce-scatter.4.cloned.1.call-done = f32[128,3]{1,0:T(8,128)} async-done(((f32[512,3]{1,0:T(8,128)}), f32[128,3]{1,0:T(8,128)}) %reduce-scatter.4.cloned.1.call-update) | async-done | bytes 1552
  352.7 4.1 %reshape.213 = bf16[512,25,32]{2,1,0:T(8,128)(2,1)} reshape(bf16[4,2,51200]{2,1,0:T(2,128)(2,1)S(1)} %all-to-all-done.3) | data formatting | bytes 1638400
  356.8 5.2 %copy.220 = bf16[25,32,4,128]{3,2,1,0:T(4,128)(2,1)S(1)} copy(bf16[25,32,4,128]{1,0,3,2:T(8,128)(2,1)} %bitcast.290) | data formatting | bytes 1638400 | tf_op jit(solution)/shard_map/all_to_all | solution.py:243
  (243 shorter events, 80.6 us)
Async XLA Ops:
  7.2 1.1 copy-start
  7.2 12.6 %copy-start.5 = (bf16[25,128,128]{2,1,0:T(8,128)(2,1)S(1)}, bf16[25,128,128]{2,1,0:T(8,128)(2,1)}, u32[]{:S(2)}) copy-start(bf16[25,128,128]{2,1,0:T(8,128)(2,1)} %param.17) | copy-start | bytes 2457604
  7.2 9.8 %copy-start.12 = (f32[3,512]{1,0:T(4,128)S(1)}, f32[3,512]{1,0:T(4,128)}, u32[]{:S(2)}) copy-start(f32[3,512]{1,0:T(4,128)} %param.18) | copy-start | bytes 18436
  7.2 12.5 %copy-start.11 = (bf16[5,128,128]{2,1,0:T(8,128)(2,1)S(1)}, bf16[5,128,128]{2,1,0:T(8,128)(2,1)}, u32[]{:S(2)}) copy-start(bf16[5,128,128]{2,1,0:T(8,128)(2,1)} %param.21) | copy-start | bytes 491524
  9.3 11.7 %copy-start.8 = (bf16[25,128,128]{2,1,0:T(8,128)(2,1)S(1)}, bf16[25,128,128]{2,1,0:T(8,128)(2,1)}, u32[]{:S(2)}) copy-start(bf16[25,128,128]{2,1,0:T(8,128)(2,1)} %param.27) | copy-start | bytes 2457604
  9.3 11.7 %copy-start.9 = (bf16[5,128,128]{2,1,0:T(8,128)(2,1)S(1)}, bf16[5,128,128]{2,1,0:T(8,128)(2,1)}, u32[]{:S(2)}) copy-start(bf16[5,128,128]{2,1,0:T(8,128)(2,1)} %param.22) | copy-start | bytes 491524
  10.7 20.8 %all-to-all-start = ((bf16[2,1024,128]{2,0,1:T(2,128)(2,1)}), bf16[2,1024,128]{2,0,1:T(2,128)(2,1)S(1)}, u32[]{:S(2)}, u32[]{:S(2)}) async-start(bf16[2,1024,128]{2,0,1:T(2,128)(2,1)} %copy.174), calls=%async_computation | async-start | bytes 1048576 | tf_op jit(solution)/shard_map/all_to_all | solution.py:213
  17.0 58.9 %collective-permute-start.2 = (f32[3,256]{1,0:T(4,128)S(1)}, f32[3,256]{1,0:T(4,128)S(1)}, u32[]{:S(2)}, u32[]{:S(2)}) collective-permute-start(f32[3,256]{1,0:T(4,128)S(1)} %get-tuple-element.313), channel_id=1, source_target_pairs={{0,4},{4,8},{8,12},{12,16},{16,20},{20,24},{24,28},{28,0},{1,5},{5... | collective-permute-start | bytes 9224 | tf_op jit(solution)/shard_map/ppermute | solution.py:25
  17.1 58.9 %collective-permute-start.3 = (f32[3,256]{1,0:T(4,128)S(1)}, f32[3,256]{1,0:T(4,128)S(1)}, u32[]{:S(2)}, u32[]{:S(2)}) collective-permute-start(f32[3,256]{1,0:T(4,128)S(1)} %get-tuple-element.314), channel_id=1, source_target_pairs={{4,0},{8,4},{12,8},{16,12},{20,16},{24,20},{28,24},{0,28},{5,1},{9... | collective-permute-start | bytes 9224 | tf_op jit(solution)/shard_map/ppermute | solution.py:26
  23.3 14.3 %copy-start.7 = (f32[64,25,25]{0,2,1:T(8,128)S(1)}, f32[64,25,25]{0,2,1:T(8,128)}, u32[]{:S(2)}) copy-start(f32[64,25,25]{0,2,1:T(8,128)} %param.23) | copy-start | bytes 480004
  31.5 29.6 %all-to-all-start.1 = ((bf16[25,128,128]{2,0,1:T(8,128)(2,1)}), bf16[25,128,128]{2,0,1:T(8,128)(2,1)}, u32[]{:S(2)}, u32[]{:S(2)}) async-start(bf16[25,128,128]{2,0,1:T(8,128)(2,1)} %copy.181), calls=%async_computation.1 | async-start | bytes 2097152 | tf_op jit(solution)/shard_map/all_to_all | solution.py:214
  40.6 24.0 %copy-start.13 = (s32[8,8]{1,0:T(8,128)S(1)}, s32[8,8]{1,0:T(8,128)}, u32[]{:S(2)}) copy-start(s32[8,8]{1,0:T(8,128)} %param.25) | copy-start | bytes 772
  61.1 28.8 %all-to-all-start.2 = ((bf16[25,128,128]{2,0,1:T(8,128)(2,1)}), bf16[25,128,128]{2,0,1:T(8,128)(2,1)S(1)}, u32[]{:S(2)}, u32[]{:S(2)}) async-start(bf16[25,128,128]{2,0,1:T(8,128)(2,1)} %copy.188), calls=%async_computation.2 | async-start | bytes 2097152 | tf_op jit(solution)/shard_map/all_to_all | solution.py:215
  67.7 3.9 %copy-start.15 = (s32[8]{0:T(128)S(1)}, s32[8]{0:T(128)}, u32[]{:S(2)}) copy-start(s32[8]{0:T(128)} %param.26) | copy-start | bytes 100
  67.8 6.4 %copy-start.14 = (s32[8]{0:T(128)S(1)}, s32[8]{0:T(128)}, u32[]{:S(2)}) copy-start(s32[8]{0:T(128)} %param.24) | copy-start | bytes 100
  68.9 7.0 %copy-start.16 = (f32[16]{0:T(128)S(1)}, f32[16]{0:T(128)}, u32[]{:S(2)}) copy-start(f32[16]{0:T(128)} %param.19) | copy-start | bytes 196
  68.9 23.3 %collective-permute-start = (bf16[1056,256]{1,0:T(8,128)(2,1)}, bf16[1056,256]{1,0:T(8,128)(2,1)}, u32[]{:S(2)}, u32[]{:S(2)}) collective-permute-start(bf16[1056,256]{1,0:T(8,128)(2,1)} %get-tuple-element.307), channel_id=1, source_target_pairs={{0,4},{4,8},{8,12},{12,16},{16,20},{20,24},{24,28},{28,0},{1,5},{5... | collective-permute-start | bytes 1622024 | tf_op jit(solution)/shard_map/ppermute | solution.py:25
  68.9 23.3 %collective-permute-start.1 = (bf16[1056,256]{1,0:T(8,128)(2,1)}, bf16[1056,256]{1,0:T(8,128)(2,1)}, u32[]{:S(2)}, u32[]{:S(2)}) collective-permute-start(bf16[1056,256]{1,0:T(8,128)(2,1)} %get-tuple-element.308), channel_id=1, source_target_pairs={{4,0},{8,4},{12,8},{16,12},{20,16},{24,20},{28,24},{0,28},{5,1},{9... | collective-permute-start | bytes 1622024 | tf_op jit(solution)/shard_map/ppermute | solution.py:26
  106.0 4.9 %copy-start.3 = (bf16[4,64,16,64]{3,1,2,0:T(8,128)(2,1)}, bf16[4,64,16,64]{3,1,2,0:T(8,128)(2,1)S(1)}, u32[]{:S(2)}) copy-start(bf16[4,64,16,64]{3,1,2,0:T(8,128)(2,1)S(1)} %get-tuple-element.475) | copy-start | bytes 1572868 | tf_op jit(solution)/shard_map/while
  127.6 1.9 copy-start.2
  132.7 23.2 %copy-start.4 = (bf16[4,64,16,64]{3,1,2,0:T(8,128)(2,1)S(1)}, bf16[4,64,16,64]{3,1,2,0:T(8,128)(2,1)}, u32[]{:S(2)}) copy-start(bf16[4,64,16,64]{3,1,2,0:T(8,128)(2,1)} %copy-done.3) | copy-start | bytes 1572868 | tf_op jit(solution)/shard_map/while
  156.0 4.9 %copy-start.3 = (bf16[4,64,16,64]{3,1,2,0:T(8,128)(2,1)}, bf16[4,64,16,64]{3,1,2,0:T(8,128)(2,1)S(1)}, u32[]{:S(2)}) copy-start(bf16[4,64,16,64]{3,1,2,0:T(8,128)(2,1)S(1)} %get-tuple-element.475) | copy-start | bytes 1572868 | tf_op jit(solution)/shard_map/while
  177.6 1.9 copy-start.2
  182.7 23.2 %copy-start.4 = (bf16[4,64,16,64]{3,1,2,0:T(8,128)(2,1)S(1)}, bf16[4,64,16,64]{3,1,2,0:T(8,128)(2,1)}, u32[]{:S(2)}) copy-start(bf16[4,64,16,64]{3,1,2,0:T(8,128)(2,1)} %copy-done.3) | copy-start | bytes 1572868 | tf_op jit(solution)/shard_map/while
  206.0 4.9 %copy-start.3 = (bf16[4,64,16,64]{3,1,2,0:T(8,128)(2,1)}, bf16[4,64,16,64]{3,1,2,0:T(8,128)(2,1)S(1)}, u32[]{:S(2)}) copy-start(bf16[4,64,16,64]{3,1,2,0:T(8,128)(2,1)S(1)} %get-tuple-element.475) | copy-start | bytes 1572868 | tf_op jit(solution)/shard_map/while
  227.6 1.9 copy-start.2
  232.7 23.2 %copy-start.4 = (bf16[4,64,16,64]{3,1,2,0:T(8,128)(2,1)S(1)}, bf16[4,64,16,64]{3,1,2,0:T(8,128)(2,1)}, u32[]{:S(2)}) copy-start(bf16[4,64,16,64]{3,1,2,0:T(8,128)(2,1)} %copy-done.3) | copy-start | bytes 1572868 | tf_op jit(solution)/shard_map/while
  256.0 4.9 %copy-start.3 = (bf16[4,64,16,64]{3,1,2,0:T(8,128)(2,1)}, bf16[4,64,16,64]{3,1,2,0:T(8,128)(2,1)S(1)}, u32[]{:S(2)}) copy-start(bf16[4,64,16,64]{3,1,2,0:T(8,128)(2,1)S(1)} %get-tuple-element.475) | copy-start | bytes 1572868 | tf_op jit(solution)/shard_map/while
  277.6 1.9 copy-start.2
  282.8 23.2 %copy-start.4 = (bf16[4,64,16,64]{3,1,2,0:T(8,128)(2,1)S(1)}, bf16[4,64,16,64]{3,1,2,0:T(8,128)(2,1)}, u32[]{:S(2)}) copy-start(bf16[4,64,16,64]{3,1,2,0:T(8,128)(2,1)} %copy-done.3) | copy-start | bytes 1572868 | tf_op jit(solution)/shard_map/while
  320.8 11.1 %copy-start.6 = (bf16[25,128,128]{2,1,0:T(8,128)(2,1)S(1)}, bf16[25,128,128]{2,1,0:T(8,128)(2,1)}, u32[]{:S(2)}) copy-start(bf16[25,128,128]{2,1,0:T(8,128)(2,1)} %param.17) | copy-start | bytes 2457604
  320.8 31.9 %all-to-all-start.3 = ((bf16[4,2,51200]{2,1,0:T(2,128)(2,1)}), bf16[4,2,51200]{2,1,0:T(2,128)(2,1)S(1)}, u32[]{:S(2)}, u32[]{:S(2)}) async-start(bf16[4,2,51200]{2,1,0:T(2,128)(2,1)} %reshape.212), calls=%async_computation.3 | async-start | bytes 1638400 | tf_op jit(solution)/shard_map/all_to_all | solution.py:243
  324.4 26.8 %reduce-scatter.4.cloned.1.call-start = ((), (), s32[]{:S(2)}) async-start(), calls=%async_computation.5 | async-start | bytes 327680
  325.3 2.5 collective-permute-start.4
  326.4 3.9 %collective-permute-start.5 = (f32[3,256]{1,0:T(4,128)S(1)}, f32[3,256]{1,0:T(4,128)S(1)}, u32[]{:S(2)}, u32[]{:S(2)}) collective-permute-start(f32[3,256]{1,0:T(4,128)S(1)} %get-tuple-element.311), channel_id=1, source_target_pairs={{0,4},{4,8},{8,12},{12,16},{16,20},{20,24},{24,28},{28,0},{1,5},{5... | collective-permute-start | bytes 9224 | tf_op jit(solution)/shard_map/ppermute | solution.py:33
  356.8 5.6 %copy-start.10 = (bf16[5,128,128]{2,1,0:T(8,128)(2,1)S(1)}, bf16[5,128,128]{2,1,0:T(8,128)(2,1)}, u32[]{:S(2)}) copy-start(bf16[5,128,128]{2,1,0:T(8,128)(2,1)} %param.22) | copy-start | bytes 491524
  363.5 2.0 copy-start.1
Sparse Core Ops, SparseCore 0:
  332.0 19.1 reduce-scatter.3
where the time goes:
time: 375 us; the launch traced here: 372 us
  local copies, waits for them, and re-layouts  201 us (54%)
  waiting for transfers between devices  60.1 us (16%)
  matrix products  45.4 us (12%)
  starting transfers between devices  24.3 us (6%)
  other arithmetic  18.4 us (5%)
  between operations  14.6 us (4%)
  loops' own time  8.68 us (2%)
    dynamic_update_slice x8, local copies, waits for them, and re-layouts, group_step(): lax.dynamic_update_slice_in_dim(attended_all, attended, begin_at, 3)  85.9 us
    unnamed x39, local copies, waits for them, and re-layouts  21.9 us
    gather x4, local copies, waits for them, and re-layouts, group_step(): value_group = jnp.take(value_blocks, slot_blocks, axis=3)  21 us
    unnamed x2, waiting for transfers between devices  18.3 us
    all_to_all x1, waiting for transfers between devices, on_device(): lax.all_to_all(values, 'head', split_axis=1, concat_axis=2, tiled=True)  18.1 us
    dot_general x4, matrix products, group_step(): jnp.einsum('khdgi,khdgsj->hgisj', rotated, value_group, preferred_element...  16.7 us
    all_to_all x1, waiting for transfers between devices, on_device(): lax.all_to_all(grads, 'head', split_axis=1, concat_axis=2, tiled=True)  11.6 us
    reshape x2, local copies, waits for them, and re-layouts, attend(): attended_all.reshape(COMP, heads_here * head_width, query_blocks_count *...  9.53 us
  transfers between devices with their start and end apart: 11, of which 6 were waited for; matrix products, arithmetic and copies ran while one was open for 8% of the time, Pallas kernels for 0%

commit v1 on v0

--- a/solution.py
+++ b/solution.py
@@ -13,6 +13,29 @@
 REACH = 4
 NFRAME = 64
 NEG_FILL = -1e30
+
+
+def cut_along(shard, dim, peers):
+    before, after = (shard.shape[:dim], shard.shape[dim + 1 :])
+    return jnp.moveaxis(shard.reshape(*before, peers, -1, *after), dim, 0)
+
+
+def joined_along(blocks, dim):
+    blocks = jnp.moveaxis(blocks, 0, dim)
+    shape = blocks.shape
+    return blocks.reshape(*shape[:dim], shape[dim] * shape[dim + 1], *shape[dim + 2 :])
+
+
+def sent_to_each(array, axis, split_dim, concat_dim):
+    peers, mine = (lax.axis_size(axis), lax.axis_index(axis))
+    tiles = cut_along(array, split_dim, peers)
+    whole = tiles
+    for lap in range(1, peers):
+        target, source = ((mine + lap) % peers, (mine - lap) % peers)
+        sent = lax.dynamic_index_in_dim(tiles, target, 0)
+        other = lax.ppermute(sent, axis, [(i, (i + lap) % peers) for i in range(peers)])
+        whole = lax.dynamic_update_slice_in_dim(whole, other, source, axis=0)
+    return joined_along(whole, concat_dim)
 
 
 def extended(shard, sides, width):
@@ -211,7 +234,7 @@
     paired = queries_keys.reshape(2, query_rows, atoms_here)
     paired_heads, values_heads, grads_heads = (
         lax.all_to_all(paired, "head", split_axis=1, concat_axis=2, tiled=True),
-        lax.all_to_all(values, "head", split_axis=1, concat_axis=2, tiled=True),
+        sent_to_each(values, "head", 1, 2),
         lax.all_to_all(grads, "head", split_axis=1, concat_axis=2, tiled=True),
     )
     packed = jnp.concatenate([paired_heads[1], values_heads.reshape(-1, dom_atoms)], 0)

time: 375 us -> 409 us (1.091)
  local copies, waits for them, and re-layouts: 201 us -> 229 us
  waiting for transfers between devices: 60.1 us -> 51 us
  matrix products: 45.4 us -> 54.3 us
    dynamic_update_slice x0 -> x3, local copies, waits for them, and re-layouts: none -> 30.5 us  [sent_to_each(): whole = lax.dynamic_update_slice_in_dim(whole, other, source, axis=0)]
    all_to_all x1 -> x0, waiting for transfers between devices: 18.1 us -> none  [on_device(): lax.all_to_all(values, 'head', split_axis=1, concat_axis=2, tiled=True)]
    all_to_all x1, waiting for transfers between devices: 8.21 us -> 24.3 us  [on_device(): lax.all_to_all(paired, 'head', split_axis=1, concat_axis=2, tiled=True)]
    all_to_all x1, waiting for transfers between devices: 11.6 us -> 0.01 us  [on_device(): lax.all_to_all(grads, 'head', split_axis=1, concat_axis=2, tiled=True)]
    ppermute x0 -> x3, starting transfers between devices: none -> 6.99 us  [sent_to_each(): lax.ppermute(sent, axis, [(i, (i + lap) % peers) for i in range(peers)])]
    dot_general x5, matrix products: 1 us -> 5.48 us  [mix_degrees(): jnp.einsum('koa,co->kca', sliced, weights[degree], preferred_element_type...]
    dot_general x10, matrix products: 2.36 us -> 6.78 us  [mix_degrees(): jnp.einsum('kca,co->koa', sliced, weights[degree], preferred_element_type...]
    all_to_all x1 -> x0, starting transfers between devices: 4.26 us -> none  [on_device(): lax.all_to_all(values, 'head', split_axis=1, concat_axis=2, tiled=True)]
  transfers between devices with their start and end apart: 11 -> 13, of which waited for: 6 -> 5; matrix products, arithmetic and copies ran while one was open for 8% -> 15% of each run, Pallas kernels for 0% -> 0%
where the time goes in v1:
time: 409 us; the launch traced here: 403 us
  local copies, waits for them, and re-layouts  229 us (56%)
  matrix products  54.3 us (13%)
  waiting for transfers between devices  51 us (12%)
  starting transfers between devices  27.7 us (7%)
  other arithmetic  18.4 us (4%)
  between operations  14.7 us (4%)
  loops' own time  8.68 us (2%)
    dynamic_update_slice x8, local copies, waits for them, and re-layouts, group_step(): lax.dynamic_update_slice_in_dim(attended_all, attended, begin_at, 3)  85.8 us
    dynamic_update_slice x3, local copies, waits for them, and re-layouts, sent_to_each(): whole = lax.dynamic_update_slice_in_dim(whole, other, source, axis=0)  30.5 us
    all_to_all x1, waiting for transfers between devices, on_device(): lax.all_to_all(paired, 'head', split_axis=1, concat_axis=2, tiled=True)  24.3 us
    unnamed x37, local copies, waits for them, and re-layouts  21.2 us
    gather x4, local copies, waits for them, and re-layouts, group_step(): value_group = jnp.take(value_blocks, slot_blocks, axis=3)  21 us
    unnamed x2, waiting for transfers between devices  19.1 us
    dot_general x4, matrix products, group_step(): jnp.einsum('khdgi,khdgsj->hgisj', rotated, value_group, preferred_element...  16.7 us
    reshape x2, local copies, waits for them, and re-layouts, attend(): attended_all.reshape(COMP, heads_here * head_width, query_blocks_count *...  9.54 us
  transfers between devices with their start and end apart: 13, of which 5 were waited for; matrix products, arithmetic and copies ran while one was open for 15% of the time, Pallas kernels for 0%

profile of v1, /device:TPU:0, one launch (start us, length us, event | category | flops | bytes accessed | tf_op | source)
XLA Modules:
  0.0 403.4 jit_solution(14868410739931379946)
XLA Ops:
  14.3 2.4 dynamic-slice_bitcast_fusion
  16.8 3.0 collective-permute-start
  19.8 2.6 collective-permute-start.1
  26.2 3.5 all-to-all-start
  29.8 2.6 collective-permute-start.6
  40.6 1.8 copy.209
  42.5 2.4 convolution_bitcast_fusion.1
  44.9 24.3 %all-to-all-done = bf16[2,1024,128]{2,0,1:T(2,128)(2,1)S(1)} async-done(((bf16[2,1024,128]{2,0,1:T(2,128)(2,1)}), bf16[2,1024,128]{2,0,1:T(2,128)(2,1)S(1)}, u32[]{:S(2)}, u32[]{:S(2)}) %all-to-all-start) | async-done | bytes 524320 | tf_op jit(solution)/shard_map/all_to_all | solution.py:236
  69.2 4.3 %all-to-all-start.1 = ((bf16[25,128,128]{2,0,1:T(8,128)(2,1)}), bf16[25,128,128]{2,0,1:T(8,128)(2,1)}, u32[]{:S(2)}, u32[]{:S(2)}) async-start(bf16[25,128,128]{2,0,1:T(8,128)(2,1)} %copy.212), calls=%async_computation.1 | async-start | bytes 2097152 | tf_op jit(solution)/shard_map/all_to_all | solution.py:238
  73.5 10.2 %dynamic_update_slice.15 = bf16[4,25,32,128]{3,0,2,1:T(4,128)(2,1)S(1)} dynamic-update-slice(bf16[4,25,32,128]{3,0,2,1:T(4,128)(2,1)S(1)} %bitcast.298, bf16[1,25,32,128]{3,0,2,1:T(2,128)(2,1)} %collective-permute-done, s32[]{:T(128)S(6)} %select_n.101, s32[]{:T(128)} %constant.183.clone.1, s32[]{:T(128)} %constant.183.clone.1, s32[]{:T(128)} %constant.183.clone.1) | dynamic-update-slice | bytes 409604 | tf_op jit(solution)/shard_map/dynamic_update_slice | solution.py:37
  83.7 10.2 %dynamic_update_slice.16 = bf16[4,25,32,128]{3,0,2,1:T(4,128)(2,1)S(1)} dynamic-update-slice(bf16[4,25,32,128]{3,0,2,1:T(4,128)(2,1)S(1)} %dynamic_update_slice.15, bf16[1,25,32,128]{3,0,2,1:T(2,128)(2,1)} %collective-permute-done.1, s32[]{:T(128)S(6)} %select_n.105, s32[]{:T(128)} %constant.183.clone.1, s32[]{:T(128)} %constant.183.clone.1, s32[]{:T(128)} %constant.183.clone.1) | dynamic-update-slice | bytes 409604 | tf_op jit(solution)/shard_map/dynamic_update_slice | solution.py:37
  93.9 10.2 %dynamic_update_slice.17 = bf16[4,25,32,128]{3,0,2,1:T(4,128)(2,1)S(1)} dynamic-update-slice(bf16[4,25,32,128]{3,0,2,1:T(4,128)(2,1)S(1)} %dynamic_update_slice.16, bf16[1,25,32,128]{3,0,2,1:T(2,128)(2,1)} %collective-permute-done.2, s32[]{:T(128)S(6)} %select_n.109, s32[]{:T(128)} %constant.183.clone.1, s32[]{:T(128)} %constant.183.clone.1, s32[]{:T(128)} %constant.183.clone.1) | dynamic-update-slice | bytes 409604 | tf_op jit(solution)/shard_map/dynamic_update_slice | solution.py:37
  105.7 2.6 collective-permute-start.4
  112.4 1.9 copy.293
  115.9 3.7 collective-permute-done.3
  123.2 3.4 reshape_reshape.7
  126.6 5.2 %copy.214 = bf16[25,4,8,16,64]{4,2,3,1,0:T(8,128)(2,1)} copy(bf16[25,4,8,16,64]{4,3,2,1,0:T(8,128)(2,1)} %reshape_reshape.7) | data formatting | bytes 3276800
  131.8 1.7 broadcast_in_dim.78.clone
  133.4 200.0 %while.17 = (s32[]{:T(128)}, bf16[25,4,8,8,64]{4,3,2,1,0:T(8,128)(2,1)}, f32[3,8,64]{2,1,0:T(8,128)S(1)}, f32[3,16,64]{2,1,0:T(8,128)S(1)}, s32[4]{0:T(128)S(1)}...) while((s32[]{:T(128)}, ...), condition=%wide.region_9.10_spmd.clone, body=%wide.region_1.9_spmd.clone.sunk | while | flops 315474432 | bytes 35243308 | solution.py:197
  142.7 1.9 constant_dynamic-slice_fusion.13
  145.6 5.3 %gather_fusion.2 = bf16[16,25,4,8,64]{4,3,2,1,0:T(8,128)(2,1)} fusion(bf16[25,4,8,16,64]{4,2,3,1,0:T(8,128)(2,1)} %get-tuple-element.475, s32[1024]{0:T(1024)S(1)} %pad_clamp_fusion.2), kind=kCustom, calls=%fused_computation.clone.clone.1 | custom fusion | bytes 3276864 | tf_op jit(solution)/shard_map/while/body/eval_jaxpr/jit(_take)/gather | solution.py:141
  150.8 4.2 %fusion.148 = (f32[4,2,64]{2,1,0:T(2,128)S(1)}, f32[4,2,64,8,64]{2,4,3,1,0:T(8,128)S(1)}, f32[4,2,64,8,64,1]{2,4,5,3,1,0:T(8,128)S(1)}) fusion(f32[4,2,64]{2,1,0:T(2,128)S(1)} %fusion.146, f32[4,2,64]{2,1,0:T(2,128)S(1)} %get-tuple-element.425, f32[2,64,8,64]{1,3,2,0:T(8,128)S(1)} %copy.316, f32[4]{0:T(128)S(1)} %get-tuple-element.479, ...), kind=kOutput, calls=%fused_computation.14.clone.1 | convolution fusion | flops 108035584 | bytes 5257264 | tf_op jit(solution)/shard_map/while/body/eval_jaxpr/khdgi,khdgsj->hgisj/dot_general | solution.py:174
  156.9 2.2 fusion.150
  160.6 21.0 %dynamic_update_slice.22 = bf16[25,4,8,8,64]{4,3,2,1,0:T(8,128)(2,1)} dynamic-update-slice(bf16[25,4,8,8,64]{4,3,2,1,0:T(8,128)(2,1)} %get-tuple-element.452, bf16[25,4,8,2,64]{4,3,2,1,0:T(2,128)(2,1)S(1)} %copy.318, s32[]{:T(128)} %constant.183.clone.1..sunk, s32[]{:T(128)} %constant.183.clone.1..sunk, s32[]{:T(128)} %constant.183.clone.1..sunk, s32[]{:T(128)S(6)} %select_n.168, ...) | dynamic-update-slice | bytes 409604 | tf_op jit(solution)/shard_map/while/body/eval_jaxpr/dynamic_update_slice | solution.py:187
  192.7 1.9 constant_dynamic-slice_fusion.13
  195.6 5.3 %gather_fusion.2 = bf16[16,25,4,8,64]{4,3,2,1,0:T(8,128)(2,1)} fusion(bf16[25,4,8,16,64]{4,2,3,1,0:T(8,128)(2,1)} %get-tuple-element.475, s32[1024]{0:T(1024)S(1)} %pad_clamp_fusion.2), kind=kCustom, calls=%fused_computation.clone.clone.1 | custom fusion | bytes 3276864 | tf_op jit(solution)/shard_map/while/body/eval_jaxpr/jit(_take)/gather | solution.py:141
  200.8 4.2 %fusion.148 = (f32[4,2,64]{2,1,0:T(2,128)S(1)}, f32[4,2,64,8,64]{2,4,3,1,0:T(8,128)S(1)}, f32[4,2,64,8,64,1]{2,4,5,3,1,0:T(8,128)S(1)}) fusion(f32[4,2,64]{2,1,0:T(2,128)S(1)} %fusion.146, f32[4,2,64]{2,1,0:T(2,128)S(1)} %get-tuple-element.425, f32[2,64,8,64]{1,3,2,0:T(8,128)S(1)} %copy.316, f32[4]{0:T(128)S(1)} %get-tuple-element.479, ...), kind=kOutput, calls=%fused_computation.14.clone.1 | convolution fusion | flops 108035584 | bytes 5257264 | tf_op jit(solution)/shard_map/while/body/eval_jaxpr/khdgi,khdgsj->hgisj/dot_general | solution.py:174
  206.9 2.2 fusion.150
  210.6 21.0 %dynamic_update_slice.22 = bf16[25,4,8,8,64]{4,3,2,1,0:T(8,128)(2,1)} dynamic-update-slice(bf16[25,4,8,8,64]{4,3,2,1,0:T(8,128)(2,1)} %get-tuple-element.452, bf16[25,4,8,2,64]{4,3,2,1,0:T(2,128)(2,1)S(1)} %copy.318, s32[]{:T(128)} %constant.183.clone.1..sunk, s32[]{:T(128)} %constant.183.clone.1..sunk, s32[]{:T(128)} %constant.183.clone.1..sunk, s32[]{:T(128)S(6)} %select_n.168, ...) | dynamic-update-slice | bytes 409604 | tf_op jit(solution)/shard_map/while/body/eval_jaxpr/dynamic_update_slice | solution.py:187
  242.7 1.9 constant_dynamic-slice_fusion.13
  245.6 5.3 %gather_fusion.2 = bf16[16,25,4,8,64]{4,3,2,1,0:T(8,128)(2,1)} fusion(bf16[25,4,8,16,64]{4,2,3,1,0:T(8,128)(2,1)} %get-tuple-element.475, s32[1024]{0:T(1024)S(1)} %pad_clamp_fusion.2), kind=kCustom, calls=%fused_computation.clone.clone.1 | custom fusion | bytes 3276864 | tf_op jit(solution)/shard_map/while/body/eval_jaxpr/jit(_take)/gather | solution.py:141
  250.8 4.2 %fusion.148 = (f32[4,2,64]{2,1,0:T(2,128)S(1)}, f32[4,2,64,8,64]{2,4,3,1,0:T(8,128)S(1)}, f32[4,2,64,8,64,1]{2,4,5,3,1,0:T(8,128)S(1)}) fusion(f32[4,2,64]{2,1,0:T(2,128)S(1)} %fusion.146, f32[4,2,64]{2,1,0:T(2,128)S(1)} %get-tuple-element.425, f32[2,64,8,64]{1,3,2,0:T(8,128)S(1)} %copy.316, f32[4]{0:T(128)S(1)} %get-tuple-element.479, ...), kind=kOutput, calls=%fused_computation.14.clone.1 | convolution fusion | flops 108035584 | bytes 5257264 | tf_op jit(solution)/shard_map/while/body/eval_jaxpr/khdgi,khdgsj->hgisj/dot_general | solution.py:174
  256.9 2.2 fusion.150
  260.6 21.0 %dynamic_update_slice.22 = bf16[25,4,8,8,64]{4,3,2,1,0:T(8,128)(2,1)} dynamic-update-slice(bf16[25,4,8,8,64]{4,3,2,1,0:T(8,128)(2,1)} %get-tuple-element.452, bf16[25,4,8,2,64]{4,3,2,1,0:T(2,128)(2,1)S(1)} %copy.318, s32[]{:T(128)} %constant.183.clone.1..sunk, s32[]{:T(128)} %constant.183.clone.1..sunk, s32[]{:T(128)} %constant.183.clone.1..sunk, s32[]{:T(128)S(6)} %select_n.168, ...) | dynamic-update-slice | bytes 409604 | tf_op jit(solution)/shard_map/while/body/eval_jaxpr/dynamic_update_slice | solution.py:187
  292.7 1.9 constant_dynamic-slice_fusion.13
  295.6 5.3 %gather_fusion.2 = bf16[16,25,4,8,64]{4,3,2,1,0:T(8,128)(2,1)} fusion(bf16[25,4,8,16,64]{4,2,3,1,0:T(8,128)(2,1)} %get-tuple-element.475, s32[1024]{0:T(1024)S(1)} %pad_clamp_fusion.2), kind=kCustom, calls=%fused_computation.clone.clone.1 | custom fusion | bytes 3276864 | tf_op jit(solution)/shard_map/while/body/eval_jaxpr/jit(_take)/gather | solution.py:141
  300.8 4.2 %fusion.148 = (f32[4,2,64]{2,1,0:T(2,128)S(1)}, f32[4,2,64,8,64]{2,4,3,1,0:T(8,128)S(1)}, f32[4,2,64,8,64,1]{2,4,5,3,1,0:T(8,128)S(1)}) fusion(f32[4,2,64]{2,1,0:T(2,128)S(1)} %fusion.146, f32[4,2,64]{2,1,0:T(2,128)S(1)} %get-tuple-element.425, f32[2,64,8,64]{1,3,2,0:T(8,128)S(1)} %copy.316, f32[4]{0:T(128)S(1)} %get-tuple-element.479, ...), kind=kOutput, calls=%fused_computation.14.clone.1 | convolution fusion | flops 108035584 | bytes 5257264 | tf_op jit(solution)/shard_map/while/body/eval_jaxpr/khdgi,khdgsj->hgisj/dot_general | solution.py:174
  307.0 2.2 fusion.150
  310.7 21.0 %dynamic_update_slice.22 = bf16[25,4,8,8,64]{4,3,2,1,0:T(8,128)(2,1)} dynamic-update-slice(bf16[25,4,8,8,64]{4,3,2,1,0:T(8,128)(2,1)} %get-tuple-element.452, bf16[25,4,8,2,64]{4,3,2,1,0:T(2,128)(2,1)S(1)} %copy.318, s32[]{:T(128)} %constant.183.clone.1..sunk, s32[]{:T(128)} %constant.183.clone.1..sunk, s32[]{:T(128)} %constant.183.clone.1..sunk, s32[]{:T(128)S(6)} %select_n.168, ...) | dynamic-update-slice | bytes 409604 | tf_op jit(solution)/shard_map/while/body/eval_jaxpr/dynamic_update_slice | solution.py:187
  333.4 3.0 reshape.164
  336.5 6.5 %copy.221 = bf16[25,32,512]{1,0,2:T(8,128)(2,1)} copy(bf16[25,32,512]{2,1,0:T(8,128)(2,1)S(1)} %reshape.164) | data formatting | bytes 1638400 | tf_op jit(solution)/shard_map/reshape | solution.py:200
  343.0 5.3 %reshape.230 = bf16[4,2,51200]{2,1,0:T(2,128)(2,1)} reshape(bf16[512,25,32]{2,1,0:T(8,128)(2,1)} %bitcast.293) | data formatting | bytes 1638400
  348.3 5.2 %all-to-all-start.2 = ((bf16[4,2,51200]{2,1,0:T(2,128)(2,1)}), bf16[4,2,51200]{2,1,0:T(2,128)(2,1)S(1)}, u32[]{:S(2)}, u32[]{:S(2)}) async-start(bf16[4,2,51200]{2,1,0:T(2,128)(2,1)} %reshape.230), calls=%async_computation.2 | async-start | bytes 1638400 | tf_op jit(solution)/shard_map/all_to_all | solution.py:266
  354.2 2.5 collective-permute-start.7
  358.0 2.6 collective-permute-done.8
  363.2 19.1 %reduce-scatter.4.cloned.1.call-done = f32[128,3]{1,0:T(8,128)} async-done(((f32[512,3]{1,0:T(8,128)}), f32[128,3]{1,0:T(8,128)}) %reduce-scatter.4.cloned.1.call-update) | async-done | bytes 1552
  383.7 4.2 %reshape.231 = bf16[512,25,32]{2,1,0:T(8,128)(2,1)} reshape(bf16[4,2,51200]{2,1,0:T(2,128)(2,1)S(1)} %all-to-all-done.2) | data formatting | bytes 1638400
  387.9 5.2 %copy.244 = bf16[25,32,4,128]{3,2,1,0:T(4,128)(2,1)S(1)} copy(bf16[25,32,4,128]{1,0,3,2:T(8,128)(2,1)} %bitcast.294) | data formatting | bytes 1638400 | tf_op jit(solution)/shard_map/all_to_all | solution.py:266
  (250 shorter events, 92.2 us)
Async XLA Ops:
  7.2 16.6 %copy-start = (bf16[128,2048]{1,0:T(8,128)(2,1)S(1)}, bf16[128,2048]{1,0:T(8,128)(2,1)}, u32[]{:S(2)}) copy-start(bf16[128,2048]{1,0:T(8,128)(2,1)} %param.20) | copy-start | bytes 1572868
  16.7 12.9 %copy-start.9 = (f32[3,512]{1,0:T(4,128)S(1)}, f32[3,512]{1,0:T(4,128)}, u32[]{:S(2)}) copy-start(f32[3,512]{1,0:T(4,128)} %param.18) | copy-start | bytes 18436
  16.7 15.6 %copy-start.7 = (bf16[5,128,128]{2,1,0:T(8,128)(2,1)S(1)}, bf16[5,128,128]{2,1,0:T(8,128)(2,1)}, u32[]{:S(2)}) copy-start(bf16[5,128,128]{2,1,0:T(8,128)(2,1)} %param.22) | copy-start | bytes 491524
  16.8 56.8 %collective-permute-start = (bf16[1,25,32,128]{3,0,2,1:T(2,128)(2,1)}, bf16[1,25,32,128]{3,0,2,1:T(2,128)(2,1)}, u32[]{:S(2)}, u32[]{:S(2)}) collective-permute-start(bf16[1,25,32,128]{3,0,2,1:T(2,128)(2,1)} %get-tuple-element.311), channel_id=1, source_target_pairs={{0,1},{1,2},{2,3},{3,0},{4,5},{5,6},{6,7},{7,4},{8,9},{9,10},{10,1... | collective-permute-start | bytes 614408 | tf_op jit(solution)/shard_map/ppermute | solution.py:36
  19.8 63.9 %collective-permute-start.1 = (bf16[1,25,32,128]{3,0,2,1:T(2,128)(2,1)}, bf16[1,25,32,128]{3,0,2,1:T(2,128)(2,1)}, u32[]{:S(2)}, u32[]{:S(2)}) collective-permute-start(bf16[1,25,32,128]{3,0,2,1:T(2,128)(2,1)} %get-tuple-element.310), channel_id=1, source_target_pairs={{0,2},{1,3},{2,0},{3,1},{4,6},{5,7},{6,4},{7,5},{8,10},{9,11},{10,... | collective-permute-start | bytes 614408 | tf_op jit(solution)/shard_map/ppermute | solution.py:36
  22.4 71.5 %collective-permute-start.2 = (bf16[1,25,32,128]{3,0,2,1:T(2,128)(2,1)}, bf16[1,25,32,128]{3,0,2,1:T(2,128)(2,1)}, u32[]{:S(2)}, u32[]{:S(2)}) collective-permute-start(bf16[1,25,32,128]{3,0,2,1:T(2,128)(2,1)} %get-tuple-element.309), channel_id=1, source_target_pairs={{0,3},{1,0},{2,1},{3,2},{4,7},{5,4},{6,5},{7,6},{8,11},{9,8},{10,9... | collective-permute-start | bytes 614408 | tf_op jit(solution)/shard_map/ppermute | solution.py:36
  26.2 43.0 %all-to-all-start = ((bf16[2,1024,128]{2,0,1:T(2,128)(2,1)}), bf16[2,1024,128]{2,0,1:T(2,128)(2,1)S(1)}, u32[]{:S(2)}, u32[]{:S(2)}) async-start(bf16[2,1024,128]{2,0,1:T(2,128)(2,1)} %copy.194), calls=%async_computation | async-start | bytes 1048576 | tf_op jit(solution)/shard_map/all_to_all | solution.py:236
  29.7 9.9 %copy-start.6 = (f32[64,25,25]{0,2,1:T(8,128)S(1)}, f32[64,25,25]{0,2,1:T(8,128)}, u32[]{:S(2)}) copy-start(f32[64,25,25]{0,2,1:T(8,128)} %param.23) | copy-start | bytes 480004
  29.7 81.3 %collective-permute-start.5 = (f32[3,256]{1,0:T(4,128)S(1)}, f32[3,256]{1,0:T(4,128)S(1)}, u32[]{:S(2)}, u32[]{:S(2)}) collective-permute-start(f32[3,256]{1,0:T(4,128)S(1)} %get-tuple-element.316), channel_id=1, source_target_pairs={{0,4},{4,8},{8,12},{12,16},{16,20},{20,24},{24,28},{28,0},{1,5},{5... | collective-permute-start | bytes 9224 | tf_op jit(solution)/shard_map/ppermute | solution.py:48
  29.8 81.2 %collective-permute-start.6 = (f32[3,256]{1,0:T(4,128)S(1)}, f32[3,256]{1,0:T(4,128)S(1)}, u32[]{:S(2)}, u32[]{:S(2)}) collective-permute-start(f32[3,256]{1,0:T(4,128)S(1)} %get-tuple-element.317), channel_id=1, source_target_pairs={{4,0},{8,4},{12,8},{16,12},{20,16},{24,20},{28,24},{0,28},{5,1},{9... | collective-permute-start | bytes 9224 | tf_op jit(solution)/shard_map/ppermute | solution.py:49
  42.5 31.0 %copy-start.10 = (s32[8,8]{1,0:T(8,128)S(1)}, s32[8,8]{1,0:T(8,128)}, u32[]{:S(2)}) copy-start(s32[8,8]{1,0:T(8,128)} %param.25) | copy-start | bytes 772
  69.2 43.2 %all-to-all-start.1 = ((bf16[25,128,128]{2,0,1:T(8,128)(2,1)}), bf16[25,128,128]{2,0,1:T(8,128)(2,1)}, u32[]{:S(2)}, u32[]{:S(2)}) async-start(bf16[25,128,128]{2,0,1:T(8,128)(2,1)} %copy.212), calls=%async_computation.1 | async-start | bytes 2097152 | tf_op jit(solution)/shard_map/all_to_all | solution.py:238
  104.3 4.1 %copy-start.12 = (s32[8]{0:T(128)S(1)}, s32[8]{0:T(128)}, u32[]{:S(2)}) copy-start(s32[8]{0:T(128)} %param.26) | copy-start | bytes 100
  104.6 4.6 %copy-start.11 = (s32[8]{0:T(128)S(1)}, s32[8]{0:T(128)}, u32[]{:S(2)}) copy-start(s32[8]{0:T(128)} %param.24) | copy-start | bytes 100
  105.7 5.2 %copy-start.13 = (f32[16]{0:T(128)S(1)}, f32[16]{0:T(128)}, u32[]{:S(2)}) copy-start(f32[16]{0:T(128)} %param.19) | copy-start | bytes 196
  105.7 13.9 %collective-permute-start.3 = (bf16[1056,256]{1,0:T(8,128)(2,1)}, bf16[1056,256]{1,0:T(8,128)(2,1)}, u32[]{:S(2)}, u32[]{:S(2)}) collective-permute-start(bf16[1056,256]{1,0:T(8,128)(2,1)} %get-tuple-element.307), channel_id=1, source_target_pairs={{0,4},{4,8},{8,12},{12,16},{16,20},{20,24},{24,28},{28,0},{1,5},{5... | collective-permute-start | bytes 1622024 | tf_op jit(solution)/shard_map/ppermute | solution.py:48
  105.7 13.9 %collective-permute-start.4 = (bf16[1056,256]{1,0:T(8,128)(2,1)}, bf16[1056,256]{1,0:T(8,128)(2,1)}, u32[]{:S(2)}, u32[]{:S(2)}) collective-permute-start(bf16[1056,256]{1,0:T(8,128)(2,1)} %get-tuple-element.308), channel_id=1, source_target_pairs={{4,0},{8,4},{12,8},{16,12},{20,16},{24,20},{28,24},{0,28},{5,1},{9... | collective-permute-start | bytes 1622024 | tf_op jit(solution)/shard_map/ppermute | solution.py:49
  133.4 4.9 %copy-start.3 = (bf16[4,64,16,64]{3,1,2,0:T(8,128)(2,1)}, bf16[4,64,16,64]{3,1,2,0:T(8,128)(2,1)S(1)}, u32[]{:S(2)}) copy-start(bf16[4,64,16,64]{3,1,2,0:T(8,128)(2,1)S(1)} %get-tuple-element.478) | copy-start | bytes 1572868 | tf_op jit(solution)/shard_map/while
  155.0 1.9 copy-start.2
  160.2 23.2 %copy-start.4 = (bf16[4,64,16,64]{3,1,2,0:T(8,128)(2,1)S(1)}, bf16[4,64,16,64]{3,1,2,0:T(8,128)(2,1)}, u32[]{:S(2)}) copy-start(bf16[4,64,16,64]{3,1,2,0:T(8,128)(2,1)} %copy-done.3) | copy-start | bytes 1572868 | tf_op jit(solution)/shard_map/while
  183.4 4.9 %copy-start.3 = (bf16[4,64,16,64]{3,1,2,0:T(8,128)(2,1)}, bf16[4,64,16,64]{3,1,2,0:T(8,128)(2,1)S(1)}, u32[]{:S(2)}) copy-start(bf16[4,64,16,64]{3,1,2,0:T(8,128)(2,1)S(1)} %get-tuple-element.478) | copy-start | bytes 1572868 | tf_op jit(solution)/shard_map/while
  205.0 1.9 copy-start.2
  210.2 23.2 %copy-start.4 = (bf16[4,64,16,64]{3,1,2,0:T(8,128)(2,1)S(1)}, bf16[4,64,16,64]{3,1,2,0:T(8,128)(2,1)}, u32[]{:S(2)}) copy-start(bf16[4,64,16,64]{3,1,2,0:T(8,128)(2,1)} %copy-done.3) | copy-start | bytes 1572868 | tf_op jit(solution)/shard_map/while
  233.4 4.9 %copy-start.3 = (bf16[4,64,16,64]{3,1,2,0:T(8,128)(2,1)}, bf16[4,64,16,64]{3,1,2,0:T(8,128)(2,1)S(1)}, u32[]{:S(2)}) copy-start(bf16[4,64,16,64]{3,1,2,0:T(8,128)(2,1)S(1)} %get-tuple-element.478) | copy-start | bytes 1572868 | tf_op jit(solution)/shard_map/while
  255.0 1.9 copy-start.2
  260.2 23.2 %copy-start.4 = (bf16[4,64,16,64]{3,1,2,0:T(8,128)(2,1)S(1)}, bf16[4,64,16,64]{3,1,2,0:T(8,128)(2,1)}, u32[]{:S(2)}) copy-start(bf16[4,64,16,64]{3,1,2,0:T(8,128)(2,1)} %copy-done.3) | copy-start | bytes 1572868 | tf_op jit(solution)/shard_map/while
  283.4 4.9 %copy-start.3 = (bf16[4,64,16,64]{3,1,2,0:T(8,128)(2,1)}, bf16[4,64,16,64]{3,1,2,0:T(8,128)(2,1)S(1)}, u32[]{:S(2)}) copy-start(bf16[4,64,16,64]{3,1,2,0:T(8,128)(2,1)S(1)} %get-tuple-element.478) | copy-start | bytes 1572868 | tf_op jit(solution)/shard_map/while
  305.0 1.9 copy-start.2
  310.2 23.2 %copy-start.4 = (bf16[4,64,16,64]{3,1,2,0:T(8,128)(2,1)S(1)}, bf16[4,64,16,64]{3,1,2,0:T(8,128)(2,1)}, u32[]{:S(2)}) copy-start(bf16[4,64,16,64]{3,1,2,0:T(8,128)(2,1)} %copy-done.3) | copy-start | bytes 1572868 | tf_op jit(solution)/shard_map/while
  348.3 13.9 %copy-start.5 = (bf16[25,128,128]{2,1,0:T(8,128)(2,1)S(1)}, bf16[25,128,128]{2,1,0:T(8,128)(2,1)}, u32[]{:S(2)}) copy-start(bf16[25,128,128]{2,1,0:T(8,128)(2,1)} %param.17) | copy-start | bytes 2457604
  348.3 35.5 %all-to-all-start.2 = ((bf16[4,2,51200]{2,1,0:T(2,128)(2,1)}), bf16[4,2,51200]{2,1,0:T(2,128)(2,1)S(1)}, u32[]{:S(2)}, u32[]{:S(2)}) async-start(bf16[4,2,51200]{2,1,0:T(2,128)(2,1)} %reshape.230), calls=%async_computation.2 | async-start | bytes 1638400 | tf_op jit(solution)/shard_map/all_to_all | solution.py:266
  353.4 28.8 %reduce-scatter.4.cloned.1.call-start = ((), (), s32[]{:S(2)}) async-start(), calls=%async_computation.4 | async-start | bytes 327680
  354.2 3.8 collective-permute-start.7
  356.7 3.9 collective-permute-start.8
  387.9 5.6 %copy-start.8 = (bf16[5,128,128]{2,1,0:T(8,128)(2,1)S(1)}, bf16[5,128,128]{2,1,0:T(8,128)(2,1)}, u32[]{:S(2)}) copy-start(bf16[5,128,128]{2,1,0:T(8,128)(2,1)} %param.22) | copy-start | bytes 491524
  394.6 2.0 copy-start.1
Sparse Core Ops, SparseCore 0:
  362.3 19.9 reduce-scatter.3
